TPU v7x, 512 devices: a whole 4x4x16 slice. The times are simulated.
512 devices in a mesh: prow: 16 (over y_hi, x, core), pcol: 32 (over y_lo, z).
Axes of the slice: x: 4, y: 4 (y_hi: 2, y_lo: 2; y = y_hi * 2 + y_lo), z: 16, core: 2. Of those that a mesh axis runs over, the one named last changes fastest.
Arguments:
- sep_inverse: bfloat16 [2, 16, 256, 1, 32, 256], P(None, 'prow', None, None, 'pcol'), may hold values from -2 to 30, as said below
- panels: bfloat16 [4, 2, 16, 256, 256], P(None, None, 'prow', 'pcol'), may hold values from -0.0625 to 0.0625
- ancestors: int32 [4, 32], replicated, may hold values from 0 to 1, as said below
- window_factor: bfloat16 [6, 256, 256], replicated, may hold values from -0.1875 to 0.1875
- diag_inverse: bfloat16 [4, 256, 256], replicated, may hold values from -1 to 4, as said below
Outputs:
- ys: float32 [4, 2, 16, 256, 256], P(None, None, 'prow', 'pcol')
- window_inverse: float32 [1024, 1024], P('prow', 'pcol')
Inputs may be any that keep to these rules, and one draw needn't show every extreme that they name: sep_inverse read as in the first step is symmetric. `diag_inverse`: each block is symmetric. ancestors[k + 1, t] <= ancestors[k, t]: a supernode's ancestor tiles lie among those of the one before it.
All inputs are finite; a program needn't handle non-finite values.
Results may differ from a plain program's by a relative error of at most 0.00035.
Values may be sent and summed in bfloat16 or wider, within the bound.
A program may use at most 64 MiB of HBM per device.

v0:
```python
import jax
import jax.numpy as jnp
from jax import lax
from jax.sharding import PartitionSpec as P


def broadcast(block, axis, owner):
    block = jnp.where(lax.axis_index(axis) == owner, block, jnp.zeros_like(block))
    return lax.psum(block, axis)


def product(operand_left, operand_right):
    return jnp.dot(
        operand_left,
        operand_right,
        precision=lax.Precision.HIGHEST,
        preferred_element_type=jnp.float32,
    )


def pair_index(earlier, later):
    return later * (later - 1) // 2 + earlier


def window_step(later, window_sums, window_factor, diag_inverse, window_blocks):
    coupled = []
    for earlier in range(later):
        running = window_sums[earlier]
        for partner in range(later):
            running = running + product(
                window_blocks[earlier, partner],
                window_factor[pair_index(partner, later)].astype(jnp.float32),
            )
        upper_block = -running
        window_blocks[earlier, later] = upper_block
        window_blocks[later, earlier] = upper_block.T
        coupled.append(upper_block)
    running = window_sums[later]
    for earlier in range(later):
        running = running + product(
            window_factor[pair_index(earlier, later)].astype(jnp.float32).T, coupled[earlier]
        )
    window_blocks[later, later] = diag_inverse[later].astype(jnp.float32) - running


def assemble_window(window_blocks, supernodes):
    return jnp.block(
        [
            [window_blocks[first, second] for second in range(supernodes)]
            for first in range(supernodes)
        ]
    )


def per_device(sep_inverse, panels, ancestors, window_factor, diag_inverse):
    prow_count = lax.axis_size("prow")
    pcol_count = lax.axis_size("pcol")
    row_index = lax.axis_index("prow")
    column_index = lax.axis_index("pcol")
    tile_rows = sep_inverse.shape[0]
    width = sep_inverse.shape[2]
    owned_count = sep_inverse.shape[3]
    supernodes = panels.shape[0]
    slice_rows = panels.shape[3]
    group_ratio = pcol_count // prow_count
    local_sep = sep_inverse.reshape(tile_rows, width, owned_count, width)
    window_blocks = {}
    columns = []
    for later in range(supernodes):
        tile_flags = lax.dynamic_slice_in_dim(
            ancestors[later].reshape(tile_rows, prow_count), row_index, 1, 1
        )
        keep_tiles = tile_flags.astype(jnp.bfloat16).reshape(tile_rows, 1, 1)
        own_piece = panels[later, :, 0] * keep_tiles
        full_rows = lax.all_gather(own_piece, "pcol", axis=1, tiled=True)
        grouped = full_rows.reshape(owned_count, group_ratio, width, width)
        picked = lax.dynamic_slice_in_dim(grouped, column_index // prow_count, 1, 1)[:, 0]
        owned_tiles = broadcast(picked, "prow", column_index % prow_count)

        def row_term(first_row, row_count, owned_tiles=owned_tiles):
            return jnp.einsum(
                "rbcd,cde->bre", local_sep, owned_tiles, preferred_element_type=jnp.float32
            )

        summed = lax.psum_scatter(
            row_term(jnp.int32(0), slice_rows * lax.axis_size("pcol")),
            "pcol",
            scatter_dimension=0,
            tiled=True,
        )
        row_total = jnp.transpose(summed, (1, 0, 2)).reshape(tile_rows * slice_rows, width)
        row_keep = jnp.repeat(
            tile_flags[:, 0].astype(jnp.float32),
            slice_rows,
            total_repeat_length=tile_rows * slice_rows,
        )
        carried = -row_total
        for earlier in range(later):
            carried = carried - product(
                columns[earlier], window_factor[pair_index(earlier, later)].astype(jnp.float32)
            )
        current = carried * row_keep[:, None]
        factor_rows = own_piece.reshape(tile_rows * slice_rows, width).astype(jnp.float32)
        window_parts = [product(columns[earlier].T, factor_rows) for earlier in range(later)]
        window_parts.append(product(factor_rows.T, current))
        window_sums = lax.psum(jnp.stack(window_parts), ("prow", "pcol"))
        window_step(later, window_sums, window_factor, diag_inverse, window_blocks)
        columns.append(current)
    ys = jnp.stack(columns).reshape(supernodes, tile_rows, 1, slice_rows, width)
    whole_window = assemble_window(window_blocks, supernodes)
    rows_each = supernodes * width // prow_count
    cols_each = supernodes * width // pcol_count
    local_window = lax.dynamic_slice(
        whole_window, (row_index * rows_each, column_index * cols_each), (rows_each, cols_each)
    )
    return (ys, local_window)


def solution(mesh):
    placed = (
        P(None, "prow", None, None, "pcol", None),
        P(None, None, "prow", "pcol", None),
        P(),
        P(),
        P(),
    )
    return jax.shard_map(
        per_device,
        mesh=mesh,
        in_specs=placed,
        out_specs=(P(None, None, "prow", "pcol", None), P("prow", "pcol")),
        check_vma=False,
    )
```

profile of v0, /device:TPU:4, one launch (start us, length us, event | category | flops | bytes accessed | tf_op | source)
XLA Modules:
  0.0 1206.1 jit_solution(4849116906709062268)
XLA Ops:
  7.3 0.8 slice_reduce_fusion.1
  8.9 0.8 bitcast_multiply_fusion.6
  9.8 70.2 %all_gather.12 = bf16[2,256,256]{2,0,1:T(2,128)(2,1)S(1)} all-gather(bf16[2,8,256]{2,0,1:T(2,128)(2,1)S(1)} %copy.58), channel_id=1, replica_groups=mesh['prow'=16,'pcol'=32] {'pcol'}, dimensions={1}, use_global_device_ids=true | all-gather | bytes 270336 | tf_op jit(solution)/shard_map/all_gather | solution.py:75
  80.4 59.8 %all_gather.13 = bf16[2,256,256]{2,0,1:T(2,128)(2,1)S(1)} all-gather(bf16[2,8,256]{2,0,1:T(2,128)(2,1)S(1)} %copy.63), channel_id=1, replica_groups=mesh['prow'=16,'pcol'=32] {'pcol'}, dimensions={1}, use_global_device_ids=true | all-gather | bytes 270336 | tf_op jit(solution)/shard_map/all_gather | solution.py:75
  142.0 61.7 %all_gather.15 = bf16[2,256,256]{2,0,1:T(2,128)(2,1)S(1)} all-gather(bf16[2,8,256]{2,0,1:T(2,128)(2,1)S(1)} %copy.73), channel_id=1, replica_groups=mesh['prow'=16,'pcol'=32] {'pcol'}, dimensions={1}, use_global_device_ids=true | all-gather | bytes 270336 | tf_op jit(solution)/shard_map/all_gather | solution.py:75
  204.8 59.8 %all_gather.14 = bf16[2,256,256]{2,0,1:T(2,128)(2,1)S(1)} all-gather(bf16[2,8,256]{2,0,1:T(2,128)(2,1)S(1)} %copy.68), channel_id=1, replica_groups=mesh['prow'=16,'pcol'=32] {'pcol'}, dimensions={1}, use_global_device_ids=true | all-gather | bytes 270336 | tf_op jit(solution)/shard_map/all_gather | solution.py:75
  265.8 141.1 %all-reduce.15.cloned.1.call-done = (bf16[256,256]{0,1:T(8,128)(2,1)}, bf16[256,256]{0,1:T(8,128)(2,1)}, bf16[256,256]{0,1:T(8,128)(2,1)}, bf16[256,256]{0,1:T(8,128)(2,1)}) async-done(((bf16[256,256]{0,1:T(8,128)(2,1)}, bf16[256,256]{0,1:T(8,128)(2,1)}, bf16[256,256]{0,1:T(8,128)(2,1)}, bf16[256,256]{0,1:T(8,128)(2,1)}), (bf16[256,256]{0,1:T(8,128)(2,1)}, bf16[256,256]{0,1:T(8,128)(2,1)}, ...) | async-done | bytes 524304 | tf_op jit(solution)/shard_map/psum | solution.py:9
  406.9 1.2 convolution_bitcast_fusion
  408.1 1.0 copy.75
  409.3 1.0 copy.60
  410.6 1.0 copy.65
  411.9 1.0 copy.70
  416.5 5.0 broadcast_select_fusion
  421.6 1.3 dynamic-slice.31
  423.5 262.1 %all-reduce.13.cloned.1.call-done = (f32[256,2,256]{2,1,0:T(2,128)}, f32[256,2,256]{2,1,0:T(2,128)}, f32[256,2,256]{2,1,0:T(2,128)}, f32[256,2,256]{2,1,0:T(2,128)}) async-done(((f32[256,2,256]{2,1,0:T(2,128)}, f32[256,2,256]{2,1,0:T(2,128)}, f32[256,2,256]{2,1,0:T(2,128)}, f32[256,2,256]{2,1,0:T(2,128)}), (f32[256,2,256]{2,1,0:T(2,128)}, f32[256,2,256]{2,1,0:T(2,128)}, f32[256,2,256]{2,1,0:T(2,128)}, ...) | async-done | bytes 2097168
  687.6 1.1 convolution_bitcast_fusion.19
  694.2 0.8 pad_maximum_fusion.2
  695.0 0.9 pad_maximum_fusion.1
  696.0 1.1 pad_maximum_fusion
  697.8 481.1 %all-reduce.11.cloned.1.call-done = (f32[1,256,256]{2,1,0:T(8,128)}, f32[4,256,256]{2,1,0:T(8,128)}, f32[2,256,256]{2,1,0:T(8,128)}, f32[3,256,256]{2,1,0:T(8,128)}) async-done(((f32[1,256,256]{2,1,0:T(8,128)}, f32[4,256,256]{2,1,0:T(8,128)}, f32[2,256,256]{2,1,0:T(8,128)}, f32[3,256,256]{2,1,0:T(8,128)}), (f32[1,256,256]{2,1,0:T(8,128)}, f32[4,256,256]{2,1,0:T(8,128)}, f32[2,256,256]{2,1,0:T(8,128)}, ...) | async-done | bytes 2621456 | tf_op jit(solution)/shard_map/psum | solution.py:106
  1178.9 1.0 subtract_bitcast_fusion
  1179.9 1.3 fusion.14
  1183.6 1.0 fusion.7
  1185.1 0.8 copy.82
  1186.7 0.9 copy.86
  1187.6 0.9 copy.91
  1189.4 1.2 fusion.6
  1190.6 0.8 copy.85
  1191.4 2.0 fusion.3
  1193.4 0.8 copy.90
  1195.8 1.9 fusion.1
  1197.9 1.1 maximum_maximum_fusion
  (108 shorter events, 24.6 us)
Async XLA Ops:
  7.2 399.7 %copy-start = (bf16[2,1,256,1,1,256]{5,2,4,3,1,0:T(8,128)(2,1)S(1)}, bf16[2,1,256,1,1,256]{5,2,4,3,1,0:T(8,128)(2,1)}, u32[]{:S(2)}) copy-start(bf16[2,1,256,1,1,256]{5,2,4,3,1,0:T(8,128)(2,1)} %param.15) | copy-start | bytes 786436
  7.2 399.7 %all-reduce.15.cloned.1.call-start = ((), (), s32[]{:S(2)}) async-start(), calls=%async_computation.2 | async-start | bytes 1048576 | tf_op jit(solution)/shard_map/psum | solution.py:9
  265.7 420.0 %all-reduce.13.cloned.1.call-start = ((), (), s32[]{:S(2)}) async-start(), calls=%async_computation.1 | async-start | bytes 4194304
  406.9 2.2 copy-start.11
  409.1 1.3 copy-start.10
  410.3 1.3 copy-start.9
  412.9 3.6 copy-start.12
  412.9 273.5 %copy-start.8 = (bf16[4,2,1,8,256]{4,3,2,1,0:T(8,128)(2,1)S(1)}, bf16[4,2,1,8,256]{4,3,2,1,0:T(8,128)(2,1)}, u32[]{:S(2)}) copy-start(bf16[4,2,1,8,256]{4,3,2,1,0:T(8,128)(2,1)} %param.16) | copy-start | bytes 98308
  412.9 277.2 %copy-start.1 = (bf16[6,256,256]{2,1,0:T(8,128)(2,1)S(1)}, bf16[6,256,256]{2,1,0:T(8,128)(2,1)}, u32[]{:S(2)}) copy-start(bf16[6,256,256]{2,1,0:T(8,128)(2,1)} %param.18) | copy-start | bytes 2359300
  412.9 765.9 %all-reduce.11.cloned.1.call-start = ((), (), s32[]{:S(2)}) async-start(), calls=%async_computation | async-start | bytes 5242880 | tf_op jit(solution)/shard_map/psum | solution.py:106
  697.1 481.8 %copy-start.7 = (bf16[4,256,256]{2,1,0:T(8,128)(2,1)S(1)}, bf16[4,256,256]{2,1,0:T(8,128)(2,1)}, u32[]{:S(2)}) copy-start(bf16[4,256,256]{2,1,0:T(8,128)(2,1)} %param.19) | copy-start | bytes 1572868
  1178.9 2.4 copy-start.6
  1179.9 1.7 copy-start.2
  1181.6 1.1 copy-start.5
  1188.4 0.9 copy-start.4
  1194.3 0.9 copy-start.3
Sparse Core Ops, SparseCore 0:
  265.8 140.9 all-reduce.14
  413.1 272.5 all-reduce.12
  697.2 481.5 all-reduce.10
where the time goes:
time: 1210 us
  waiting for transfers between devices  884 us (73%)
  blocking collectives  252 us (21%)
  local copies, waits for them, and re-layouts  20.5 us (2%)
  matrix products  19.6 us (2%)
  other arithmetic  15 us (1%)
  between operations  14.9 us (1%)
    psum x1, waiting for transfers between devices, per_device(): window_sums = lax.psum(jnp.stack(window_parts), ('prow', 'pcol'))  481 us
    unnamed x4, waiting for transfers between devices  262 us
    all_gather x4, blocking collectives, per_device(): full_rows = lax.all_gather(own_piece, 'pcol', axis=1, tiled=True)  252 us
    psum x1, waiting for transfers between devices, broadcast(): return lax.psum(block, axis)  141 us
  transfers between devices with their start and end apart: 3, of which 3 were waited for; matrix products, arithmetic and copies ran while one was open for 1% of the time, Pallas kernels for 0%

commit v1 on v0

--- a/solution.py
+++ b/solution.py
@@ -103,7 +103,7 @@
         factor_rows = own_piece.reshape(tile_rows * slice_rows, width).astype(jnp.float32)
         window_parts = [product(columns[earlier].T, factor_rows) for earlier in range(later)]
         window_parts.append(product(factor_rows.T, current))
-        window_sums = lax.psum(jnp.stack(window_parts), ("prow", "pcol"))
+        window_sums = lax.psum(lax.psum(jnp.stack(window_parts), "pcol"), axis_name="prow")
         window_step(later, window_sums, window_factor, diag_inverse, window_blocks)
         columns.append(current)
     ys = jnp.stack(columns).reshape(supernodes, tile_rows, 1, slice_rows, width)

time: 1210 us -> 1140 us (0.942)
  the two profiles are of different devices: /device:TPU:4 before, /device:TPU:7 now
where the time goes in v1:
time: 1140 us
  waiting for transfers between devices  875 us (77%)
  blocking collectives  197 us (17%)
  local copies, waits for them, and re-layouts  20.5 us (2%)
  matrix products  19.6 us (2%)
  other arithmetic  15 us (1%)
  between operations  14.9 us (1%)
    psum x1, waiting for transfers between devices, per_device(): lax.psum(jnp.stack(window_parts), 'pcol')  259 us
    unnamed x5, waiting for transfers between devices  233 us
    psum x1, waiting for transfers between devices, broadcast(): return lax.psum(block, axis)  203 us
    all_gather x4, blocking collectives, per_device(): full_rows = lax.all_gather(own_piece, 'pcol', axis=1, tiled=True)  197 us
    psum x1, waiting for transfers between devices, per_device(): lax.psum(lax.psum(jnp.stack(window_parts), 'pcol'), axis_name='prow')  180 us
  transfers between devices with their start and end apart: 4, of which 4 were waited for; matrix products, arithmetic and copies ran while one was open for 1% of the time, Pallas kernels for 0%

profile of v1, /device:TPU:7, one launch (start us, length us, event | category | flops | bytes accessed | tf_op | source)
XLA Modules:
  0.0 1141.5 jit_solution(18065701218539782110)
XLA Ops:
  7.3 0.8 slice_reduce_fusion.1
  8.9 0.8 bitcast_multiply_fusion.6
  9.8 56.2 %all_gather.12 = bf16[2,256,256]{2,0,1:T(2,128)(2,1)S(1)} all-gather(bf16[2,8,256]{2,0,1:T(2,128)(2,1)S(1)} %copy.58), channel_id=1, replica_groups=mesh['prow'=16,'pcol'=32] {'pcol'}, dimensions={1}, use_global_device_ids=true | all-gather | bytes 270336 | tf_op jit(solution)/shard_map/all_gather | solution.py:75
  66.4 46.0 %all_gather.13 = bf16[2,256,256]{2,0,1:T(2,128)(2,1)S(1)} all-gather(bf16[2,8,256]{2,0,1:T(2,128)(2,1)S(1)} %copy.63), channel_id=1, replica_groups=mesh['prow'=16,'pcol'=32] {'pcol'}, dimensions={1}, use_global_device_ids=true | all-gather | bytes 270336 | tf_op jit(solution)/shard_map/all_gather | solution.py:75
  114.2 48.3 %all_gather.15 = bf16[2,256,256]{2,0,1:T(2,128)(2,1)S(1)} all-gather(bf16[2,8,256]{2,0,1:T(2,128)(2,1)S(1)} %copy.73), channel_id=1, replica_groups=mesh['prow'=16,'pcol'=32] {'pcol'}, dimensions={1}, use_global_device_ids=true | all-gather | bytes 270336 | tf_op jit(solution)/shard_map/all_gather | solution.py:75
  163.6 46.0 %all_gather.14 = bf16[2,256,256]{2,0,1:T(2,128)(2,1)S(1)} all-gather(bf16[2,8,256]{2,0,1:T(2,128)(2,1)S(1)} %copy.68), channel_id=1, replica_groups=mesh['prow'=16,'pcol'=32] {'pcol'}, dimensions={1}, use_global_device_ids=true | all-gather | bytes 270336 | tf_op jit(solution)/shard_map/all_gather | solution.py:75
  210.8 203.1 %all-reduce.19.cloned.1.call-done = (bf16[256,256]{0,1:T(8,128)(2,1)}, bf16[256,256]{0,1:T(8,128)(2,1)}, bf16[256,256]{0,1:T(8,128)(2,1)}, bf16[256,256]{0,1:T(8,128)(2,1)}) async-done(((bf16[256,256]{0,1:T(8,128)(2,1)}, bf16[256,256]{0,1:T(8,128)(2,1)}, bf16[256,256]{0,1:T(8,128)(2,1)}, bf16[256,256]{0,1:T(8,128)(2,1)}), (bf16[256,256]{0,1:T(8,128)(2,1)}, bf16[256,256]{0,1:T(8,128)(2,1)}, ...) | async-done | bytes 524304 | tf_op jit(solution)/shard_map/psum | solution.py:9
  413.9 1.2 convolution_bitcast_fusion
  415.1 1.0 copy.75
  416.4 1.0 copy.60
  417.7 1.0 copy.65
  419.0 1.0 copy.70
  423.4 5.0 broadcast_select_fusion
  428.5 1.3 dynamic-slice.31
  430.4 232.5 %all-reduce.15.cloned.1.call-done = (f32[256,2,256]{2,1,0:T(2,128)}, f32[256,2,256]{2,1,0:T(2,128)}, f32[256,2,256]{2,1,0:T(2,128)}, f32[256,2,256]{2,1,0:T(2,128)}) async-done(((f32[256,2,256]{2,1,0:T(2,128)}, f32[256,2,256]{2,1,0:T(2,128)}, f32[256,2,256]{2,1,0:T(2,128)}, f32[256,2,256]{2,1,0:T(2,128)}), (f32[256,2,256]{2,1,0:T(2,128)}, f32[256,2,256]{2,1,0:T(2,128)}, f32[256,2,256]{2,1,0:T(2,128)}, ...) | async-done | bytes 2097168
  664.8 1.1 convolution_bitcast_fusion.19
  671.5 0.8 pad_maximum_fusion.2
  672.3 0.9 pad_maximum_fusion.1
  673.3 1.1 pad_maximum_fusion
  674.6 259.3 %all-reduce.13.cloned.1.call-done = (f32[1,256,256]{2,1,0:T(8,128)}, f32[4,256,256]{2,1,0:T(8,128)}, f32[2,256,256]{2,1,0:T(8,128)}, f32[3,256,256]{2,1,0:T(8,128)}) async-done(((f32[1,256,256]{2,1,0:T(8,128)}, f32[4,256,256]{2,1,0:T(8,128)}, f32[2,256,256]{2,1,0:T(8,128)}, f32[3,256,256]{2,1,0:T(8,128)}), (f32[1,256,256]{2,1,0:T(8,128)}, f32[4,256,256]{2,1,0:T(8,128)}, f32[2,256,256]{2,1,0:T(8,128)}, ...) | async-done | bytes 2621456 | tf_op jit(solution)/shard_map/psum | solution.py:106
  934.6 179.6 %all-reduce.17.cloned.1.call-done = (f32[1,256,256]{2,1,0:T(8,128)}, f32[4,256,256]{2,1,0:T(8,128)}, f32[2,256,256]{2,1,0:T(8,128)}, f32[3,256,256]{2,1,0:T(8,128)}) async-done(((f32[1,256,256]{2,1,0:T(8,128)}, f32[4,256,256]{2,1,0:T(8,128)}, f32[2,256,256]{2,1,0:T(8,128)}, f32[3,256,256]{2,1,0:T(8,128)}), (f32[1,256,256]{2,1,0:T(8,128)}, f32[4,256,256]{2,1,0:T(8,128)}, f32[2,256,256]{2,1,0:T(8,128)}, ...) | async-done | bytes 2621456 | tf_op jit(solution)/shard_map/psum | solution.py:106
  1114.2 1.0 subtract_bitcast_fusion
  1115.3 1.3 fusion.14
  1119.0 1.0 fusion.7
  1120.4 0.8 copy.82
  1122.1 0.9 copy.86
  1122.9 0.9 copy.91
  1124.7 1.2 fusion.6
  1126.0 0.8 copy.85
  1126.8 2.0 fusion.3
  1131.2 1.9 fusion.1
  1133.2 1.1 maximum_maximum_fusion
  (111 shorter events, 25.5 us)
Async XLA Ops:
  7.2 406.8 %copy-start = (bf16[2,1,256,1,1,256]{5,2,4,3,1,0:T(8,128)(2,1)S(1)}, bf16[2,1,256,1,1,256]{5,2,4,3,1,0:T(8,128)(2,1)}, u32[]{:S(2)}) copy-start(bf16[2,1,256,1,1,256]{5,2,4,3,1,0:T(8,128)(2,1)} %param.15) | copy-start | bytes 786436
  7.2 406.8 %all-reduce.19.cloned.1.call-start = ((), (), s32[]{:S(2)}) async-start(), calls=%async_computation.3 | async-start | bytes 1048576 | tf_op jit(solution)/shard_map/psum | solution.py:9
  210.8 452.2 %all-reduce.15.cloned.1.call-start = ((), (), s32[]{:S(2)}) async-start(), calls=%async_computation.1 | async-start | bytes 4194304
  413.9 2.2 copy-start.11
  416.1 1.3 copy-start.10
  417.4 1.3 copy-start.9
  420.0 3.4 copy-start.12
  420.0 243.7 %copy-start.8 = (bf16[4,2,1,8,256]{4,3,2,1,0:T(8,128)(2,1)S(1)}, bf16[4,2,1,8,256]{4,3,2,1,0:T(8,128)(2,1)}, u32[]{:S(2)}) copy-start(bf16[4,2,1,8,256]{4,3,2,1,0:T(8,128)(2,1)} %param.16) | copy-start | bytes 98308
  420.0 247.4 %copy-start.1 = (bf16[6,256,256]{2,1,0:T(8,128)(2,1)S(1)}, bf16[6,256,256]{2,1,0:T(8,128)(2,1)}, u32[]{:S(2)}) copy-start(bf16[6,256,256]{2,1,0:T(8,128)(2,1)} %param.18) | copy-start | bytes 2359300
  420.0 513.8 %all-reduce.13.cloned.1.call-start = ((), (), s32[]{:S(2)}) async-start(), calls=%async_computation | async-start | bytes 5242880 | tf_op jit(solution)/shard_map/psum | solution.py:106
  674.3 439.9 %all-reduce.17.cloned.1.call-start = ((), (), s32[]{:S(2)}) async-start(), calls=%async_computation.2 | async-start | bytes 5242880 | tf_op jit(solution)/shard_map/psum | solution.py:106
  933.9 180.3 %copy-start.7 = (bf16[4,256,256]{2,1,0:T(8,128)(2,1)S(1)}, bf16[4,256,256]{2,1,0:T(8,128)(2,1)}, u32[]{:S(2)}) copy-start(bf16[4,256,256]{2,1,0:T(8,128)(2,1)} %param.19) | copy-start | bytes 1572868
  1114.2 2.4 copy-start.6
  1115.3 1.7 copy-start.2
  1116.9 1.1 copy-start.5
  1123.8 0.9 copy-start.4
  1129.6 0.9 copy-start.3
Sparse Core Ops, SparseCore 0:
  210.9 203.0 all-reduce.18
  420.1 242.7 all-reduce.14
  674.5 259.3 all-reduce.12
  936.9 177.2 all-reduce.16
